TPU v7x, 32 devices: a whole 2x2x4 slice. The times are simulated.
32 devices in a mesh: wide: 8 (over z, y), narrow: 4 (over x, core).
Axes of the slice: x: 2, y: 2, z: 4, core: 2. Of those that a mesh axis runs over, the one named last changes fastest.
Arguments:
- residual: bfloat16 [8, 4, 2048, 256], P('wide', 'narrow'), may hold values from -6 to 6
- scaling: float32 [8, 4, 2048], P('wide', 'narrow'), may hold values from 0.25 to 1
- local_inverse: bfloat16 [8, 4, 2048, 2048], P('wide', 'narrow'), may hold values from -0.125 to 0.125
- coarse_basis: bfloat16 [8, 4, 24, 2048], P('wide', 'narrow'), may hold values from -0.125 to 0.125
- primal_map: int32 [8, 4, 24], P('wide', 'narrow'), may hold values from 0 to 95
- slot_index: int32 [8, 4, 6, 256], P('wide', 'narrow'), may hold values from 0 to 2047, as said below
- slot_length: int32 [8, 4, 6], P('wide', 'narrow'), may hold values from 0 to 256, as said below
- coarse_sub: float32 [8, 96, 96], P('wide'), may hold values from -0.625 to 0.625
- coarse_pivot: float32 [8, 96, 96], P('wide'), as said below
Outputs:
- interface_sum: float32 [8, 4, 2048, 256], P('wide', 'narrow')
Inputs may be any that keep to these rules, and one draw needn't show every extreme that they name: `slot_index`: within one slot of one subdomain the 256 entries are distinct. `slot_length`: paired slots have equal lengths: slot j of subdomain (w, n) and slot n of (w, j); slot 4 of (w, n) and slot 5 of (w - 1, n). A subdomain's own narrow slot n, the slot 4 of slab 0 and the slot 5 of slab 8 - 1 have length 0. `coarse_pivot`: Symmetric.
All inputs are finite; a program needn't handle non-finite values.
Results may differ from a plain program's by a relative error of at most 0.0039.
The roundings to bfloat16 on the way count: a program that leaves them out, or rounds other values in their place, can miss the bound.
Values may be sent and summed in bfloat16 or wider, within the bound.
No kernel may reach another device: no remote copies, remote signals or barrier semaphores. Data moves between devices by JAX's collectives and lax.ppermute only.
A program may use at most 128 MiB of HBM per device.

v0:
```python
import jax
import jax.numpy as jnp
from jax import lax
from jax.sharding import PartitionSpec as P

highest = lax.Precision.HIGHEST


def entering(part, axis, combine, identity, reverse):
    count = lax.axis_size(axis)
    place = lax.axis_index(axis)
    ahead = count - 1 - place if reverse else place
    gathered = jax.tree.map(lambda a: lax.all_gather(a, axis), part)
    state = jax.tree.map(lambda a, e: jnp.zeros_like(a) + jnp.asarray(e, a.dtype), part, identity)

    def one(turn, state):
        source = count - 1 - turn if reverse else turn
        return combine(
            state, jax.tree.map(lambda a: lax.dynamic_index_in_dim(a, source, 0, False), gathered)
        )

    return lax.fori_loop(0, ahead, one, state)


def shifted(block, axis, distance):
    devices = range(lax.axis_size(axis))
    route = [(i - distance, i) for i in devices if i - distance in devices]
    return lax.ppermute(block, axis, route)


def exact_dot(left, right):
    return jnp.dot(left, right, precision=highest, preferred_element_type=jnp.float32)


def compose(earlier, later):
    return (exact_dot(later[0], earlier[0]), exact_dot(later[0], earlier[1]) + later[1])


def coarse_solve(coarse_rhs, sub_block, pivot_block):
    order = sub_block.shape[0]
    identity = jnp.eye(order, dtype=jnp.float32)
    empty = jnp.zeros_like(coarse_rhs)
    sub_trans = sub_block.T
    before = entering((-sub_block, coarse_rhs), "wide", compose, (identity, empty), False)
    chain_y = coarse_rhs - exact_dot(sub_block, before[1])
    pivoted = exact_dot(pivot_block, chain_y)
    after = entering(
        (-sub_trans, exact_dot(sub_trans, pivoted)), "wide", compose, (identity, empty), True
    )
    return pivoted - after[1]


def body(
    residual,
    scaling,
    local_inverse,
    coarse_basis,
    primal_map,
    slot_index,
    slot_length,
    coarse_sub,
    coarse_pivot,
):
    groups = lax.axis_size("narrow")
    weights = scaling[0, 0]
    weighted = (weights[:, None] * residual[0, 0].astype(jnp.float32)).astype(jnp.bfloat16)
    local_part = jnp.dot(local_inverse[0, 0], weighted, preferred_element_type=jnp.float32)
    basis = coarse_basis[0, 0]
    primal = jnp.dot(basis, weighted, preferred_element_type=jnp.float32)
    order = coarse_sub.shape[1]
    one_hot = (primal_map[0, 0][:, None] == jnp.arange(order, dtype=jnp.int32)[None, :]).astype(
        jnp.float32
    )
    assembly = lax.dot_general(
        one_hot,
        primal,
        (((0,), (0,)), ((), ())),
        precision=highest,
        preferred_element_type=jnp.float32,
    )
    coarse_share = lax.psum_scatter(assembly, "narrow", scatter_dimension=1, tiled=True)
    solved_share = coarse_solve(coarse_share, coarse_sub[0], coarse_pivot[0])
    coarse_sol = lax.all_gather(solved_share, "narrow", axis=1, tiled=True)
    coarse_vals = exact_dot(one_hot, coarse_sol)
    spread = lax.dot_general(
        basis.astype(jnp.float32),
        coarse_vals,
        (((0,), (0,)), ((), ())),
        precision=highest,
        preferred_element_type=jnp.float32,
    )
    combined = (weights[:, None] * (local_part + spread)).astype(jnp.bfloat16)
    indices = slot_index[0, 0]
    lengths = slot_length[0, 0]
    capacity = indices.shape[1]
    live_mask = jnp.arange(capacity, dtype=jnp.int32)[None, :] < lengths[:, None]
    outgoing = jnp.where(live_mask[:, :, None], combined[indices], jnp.zeros((), jnp.bfloat16))
    narrow_in = lax.all_to_all(outgoing[:groups], "narrow", split_axis=0, concat_axis=0, tiled=True)
    below = shifted(outgoing[groups + 1], "wide", 1)
    above = shifted(outgoing[groups], "wide", -1)
    incoming = jnp.concatenate([narrow_in, below[None], above[None]], axis=0)
    columns = combined.shape[1]
    summed = (
        combined.astype(jnp.float32)
        .at[indices.reshape(-1)]
        .add(incoming.reshape(-1, columns).astype(jnp.float32))
    )
    return summed[None, None]


def solution(mesh):
    in_specs = (
        P("wide", "narrow", None, None),
        P("wide", "narrow", None),
        P("wide", "narrow", None, None),
        P("wide", "narrow", None, None),
        P("wide", "narrow", None),
        P("wide", "narrow", None, None),
        P("wide", "narrow", None),
        P("wide", None, None),
        P("wide", None, None),
    )
    out_specs = P("wide", "narrow", None, None)
    return jax.shard_map(body, mesh=mesh, in_specs=in_specs, out_specs=out_specs, check_vma=False)
```

profile of v0, /device:TPU:0, one launch (start us, length us, event | category | flops | bytes accessed | tf_op | source)
XLA Modules:
  0.0 194.7 jit_solution(11893826487892499667)
XLA Ops:
  6.6 0.9 copy-done
  7.5 2.1 %fusion.15 = f32[256,24]{1,0:T(8,128)S(1)} fusion(bf16[1,1,2048,256]{3,2,1,0:T(8,128)(2,1)} %param.13, f32[2048]{0:T(1024)} %bitcast.94, bf16[1,1,24,2048]{3,2,1,0:T(8,128)(2,1)S(1)} %copy-done), kind=kOutput, calls=%fused_computation.25 | convolution fusion | flops 26738688 | bytes 1179648 | tf_op jit(solution)/shard_map/dot_general | solution.py:69
  9.5 1.6 fusion.26
  11.3 32.9 %all_gather.25 = f32[8,96,96]{2,1,0:T(8,128)S(1)} all-gather(f32[1,96,96]{2,1,0:T(8,128)S(1)} %neg.10), channel_id=1, replica_groups=mesh['wide'=8,'narrow'=4] {'wide'}, dimensions={0}, use_global_device_ids=true | all-gather | bytes 331776 | tf_op jit(solution)/shard_map/all_gather | solution.py:13
  44.3 30.9 %all-gather.1 = f32[768,96]{1,0:T(8,128)S(1)} all-gather(f32[96,96]{1,0:T(8,128)S(1)} %fusion.24), channel_id=3, replica_groups=mesh['wide'=8,'narrow'=4] {'wide'}, dimensions={0}, use_global_device_ids=true | all-gather | bytes 331776 | tf_op jit(solution)/shard_map/all_gather | solution.py:13
  75.2 6.5 %fusion.6 = f32[256,2048]{1,0:T(8,128)S(1)} fusion(bf16[1,1,2048,2048]{3,2,1,0:T(8,128)(2,1)} %param.15, bf16[1,1,2048,256]{3,2,1,0:T(8,128)(2,1)} %param.13, f32[2048]{0:T(1024)S(1)} %bitcast.95), kind=kOutput, calls=%fused_computation.10 | convolution fusion | flops 2149056512 | bytes 11542528 | tf_op jit(solution)/shard_map/dot_general | solution.py:67
  81.8 30.9 %all-gather.3 = f32[8,96,64]{1,2,0:T(8,128)S(1)} all-gather(f32[1,96,64]{1,2,0:T(8,128)} %bitcast.92), channel_id=2, replica_groups=mesh['wide'=8,'narrow'=4] {'wide'}, dimensions={0}, use_global_device_ids=true | all-gather | bytes 221184 | tf_op jit(solution)/shard_map/all_gather | solution.py:13
  112.7 1.0 fusion.13
  113.7 0.2 fusion.22
  114.1 32.2 %all-gather.4 = f32[8,96,64]{1,2,0:T(8,128)S(1)} all-gather(f32[1,96,64]{1,2,0:T(8,128)S(1)} %convolution_bitcast_fusion), channel_id=4, replica_groups=mesh['wide'=8,'narrow'=4] {'wide'}, dimensions={0}, use_global_device_ids=true | all-gather | bytes 221184 | tf_op jit(solution)/shard_map/all_gather | solution.py:13
  146.4 1.8 while.27
  146.4 0.2 convolution_add_fusion.6
  146.6 0.2 convolution_add_fusion.6
  146.9 0.2 convolution_add_fusion.6
  147.1 0.2 convolution_add_fusion.6
  147.4 0.2 convolution_add_fusion.6
  147.7 0.2 convolution_add_fusion.6
  147.9 0.2 convolution_add_fusion.6
  148.2 5.4 %all_gather.32 = f32[96,256]{0,1:T(8,128)S(1)} all-gather(f32[96,64]{0,1:T(8,128)S(1)} %bitcast_subtract_fusion), channel_id=1, replica_groups=mesh['wide'=8,'narrow'=4] {'narrow'}, dimensions={1}, use_global_device_ids=true | all-gather | bytes 122880 | tf_op jit(solution)/shard_map/all_gather | solution.py:83
  153.6 0.2 fusion.25
  153.8 1.2 fusion.10
  155.0 0.5 copy.14
  155.5 4.8 %gather_fusion = bf16[1536,256]{1,0:T(8,128)(2,1)S(1)} fusion(bf16[2048,256]{1,0:T(8,128)(2,1)S(1)} %copy.14, s32[2048]{0:T(1024)S(1)} %pad_clamp_fusion), kind=kCustom, calls=%fused_computation | custom fusion | bytes 1579008 | tf_op jit(solution)/shard_map/gather | solution.py:97
  160.3 0.3 broadcast_select_fusion
  160.6 0.8 slice.14
  161.4 3.5 %all-to-all-start = ((bf16[4,256,256]{2,1,0:T(8,128)(2,1)}), bf16[4,256,256]{2,1,0:T(8,128)(2,1)S(1)}, u32[]{:S(2)}, u32[]{:S(2)}) async-start(bf16[4,256,256]{2,1,0:T(8,128)(2,1)} %slice.14), calls=%async_computation.1 | async-start | bytes 1048576 | tf_op jit(solution)/shard_map/all_to_all | solution.py:98
  164.9 3.7 %collective-permute-start = (bf16[256,256]{1,0:T(8,128)(2,1)S(1)}, bf16[256,256]{1,0:T(8,128)(2,1)S(1)}, u32[]{:S(2)}, u32[]{:S(2)}) collective-permute-start(bf16[256,256]{1,0:T(8,128)(2,1)S(1)} %get-tuple-element.155), channel_id=1, source_target_pairs={{0,4},{4,8},{8,12},{12,16},{16,20},{20,24},{24,28},{1,5},{5,9},{9,... | collective-permute-start | bytes 393224 | tf_op jit(solution)/shard_map/ppermute | solution.py:28
  168.6 1.3 collective-permute-start.1
  169.9 1.6 copy.15
  171.5 0.4 collective-permute-done
  171.9 4.1 %collective-permute-done.1 = bf16[256,256]{1,0:T(8,128)(2,1)S(1)} collective-permute-done((bf16[256,256]{1,0:T(8,128)(2,1)S(1)}, bf16[256,256]{1,0:T(8,128)(2,1)S(1)}, u32[]{:S(2)}, u32[]{:S(2)}) %collective-permute-start.1) | collective-permute-done | bytes 131104 | tf_op jit(solution)/shard_map/ppermute | solution.py:28
  176.2 11.7 %scatter_custom_fusion = f32[2048,256]{1,0:T(8,128)} fusion(f32[2048,256]{1,0:T(8,128)} %copy.15, s32[1536]{0:T(1024)S(1)} %fusion.27, bf16[1536,256]{1,0:T(8,128)(2,1)S(1)} %bitcast.87), kind=kCustom, calls=%fused_computation.17 | custom fusion | flops 786432 | bytes 2883584 | tf_op jit(solution)/shard_map/scatter-add | solution.py:106
  (39 shorter events, 0.6 us)
Async XLA Ops:
  6.5 0.9 copy-start
  6.5 68.7 %copy-start.4 = (f32[1,1,2048]{2,1,0:T(1,128)S(1)}, f32[1,1,2048]{2,1,0:T(1,128)}, u32[]{:S(2)}) copy-start(f32[1,1,2048]{2,1,0:T(1,128)} %param.14) | copy-start | bytes 24580
  6.5 4.6 %copy-start.1 = (f32[1,96,96]{2,1,0:T(8,128)S(1)}, f32[1,96,96]{2,1,0:T(8,128)}, u32[]{:S(2)}) copy-start(f32[1,96,96]{2,1,0:T(8,128)} %param.20) | copy-start | bytes 110596
  6.5 4.7 %copy-start.3 = (s32[1,1,6,256]{3,1,2,0:T(1,128)S(1)}, s32[1,1,6,256]{3,1,2,0:T(1,128)}, u32[]{:S(2)}) copy-start(s32[1,1,6,256]{3,1,2,0:T(1,128)} %param.18) | copy-start | bytes 18436
  6.5 75.3 %reduce-scatter.2.cloned.1.call-start = ((), (), s32[]{:S(2)}) async-start(), calls=%async_computation.2 | async-start | bytes 163840 | tf_op jit(solution)/shard_map/reduce_scatter | solution.py:81
  75.2 6.5 %copy-start.6 = (s32[1,1,6]{2,1,0:T(1,128)S(1)}, s32[1,1,6]{2,1,0:T(1,128)}, u32[]{:S(2)}) copy-start(s32[1,1,6]{2,1,0:T(1,128)} %param.19) | copy-start | bytes 76
  75.2 38.5 %copy-start.2 = (f32[1,96,96]{2,1,0:T(8,128)S(1)}, f32[1,96,96]{2,1,0:T(8,128)}, u32[]{:S(2)}) copy-start(f32[1,96,96]{2,1,0:T(8,128)} %param.21) | copy-start | bytes 110596
  81.7 71.9 %copy-start.5 = (s32[1,1,24]{2,1,0:T(1,128)S(1)}, s32[1,1,24]{2,1,0:T(1,128)}, u32[]{:S(2)}) copy-start(s32[1,1,24]{2,1,0:T(1,128)} %param.17) | copy-start | bytes 292
  161.4 14.7 %all-to-all-start = ((bf16[4,256,256]{2,1,0:T(8,128)(2,1)}), bf16[4,256,256]{2,1,0:T(8,128)(2,1)S(1)}, u32[]{:S(2)}, u32[]{:S(2)}) async-start(bf16[4,256,256]{2,1,0:T(8,128)(2,1)} %slice.14), calls=%async_computation.1 | async-start | bytes 1048576 | tf_op jit(solution)/shard_map/all_to_all | solution.py:98
  164.9 7.0 %collective-permute-start = (bf16[256,256]{1,0:T(8,128)(2,1)S(1)}, bf16[256,256]{1,0:T(8,128)(2,1)S(1)}, u32[]{:S(2)}, u32[]{:S(2)}) collective-permute-start(bf16[256,256]{1,0:T(8,128)(2,1)S(1)} %get-tuple-element.155), channel_id=1, source_target_pairs={{0,4},{4,8},{8,12},{12,16},{16,20},{20,24},{24,28},{1,5},{5,9},{9,... | collective-permute-start | bytes 393224 | tf_op jit(solution)/shard_map/ppermute | solution.py:28
  168.6 7.5 %collective-permute-start.1 = (bf16[256,256]{1,0:T(8,128)(2,1)S(1)}, bf16[256,256]{1,0:T(8,128)(2,1)S(1)}, u32[]{:S(2)}, u32[]{:S(2)}) collective-permute-start(bf16[256,256]{1,0:T(8,128)(2,1)S(1)} %get-tuple-element.156), channel_id=1, source_target_pairs={{4,0},{8,4},{12,8},{16,12},{20,16},{24,20},{28,24},{5,1},{9,5},{13... | collective-permute-start | bytes 393224 | tf_op jit(solution)/shard_map/ppermute | solution.py:28
Sparse Core Ops, SparseCore 0:
  11.2 22.3 reduce-scatter.1
where the time goes:
time: 195 us
  blocking collectives  132 us (68%)
  matrix products  14.4 us (7%)
  between operations  13.6 us (7%)
  other arithmetic  12.2 us (6%)
  local copies, waits for them, and re-layouts  8.77 us (4%)
  starting transfers between devices  8.46 us (4%)
  waiting for transfers between devices  4.55 us (2%)
    all_gather x4, blocking collectives, entering(): gathered = jax.tree.map(lambda a: lax.all_gather(a, axis), part)  127 us
    scatter-add x1, other arithmetic, body(): summed = combined.astype(jnp.float32).at[indices.reshape(-1)].add(incomin...  11.7 us
    dot_general x1, matrix products, body(): jnp.dot(local_inverse[0, 0], weighted, preferred_element_type=jnp.float32)  6.48 us
    all_gather x1, blocking collectives, body(): coarse_sol = lax.all_gather(solved_share, 'narrow', axis=1, tiled=True)  5.42 us
    ppermute x2, starting transfers between devices, shifted(): return lax.ppermute(block, axis, route)  4.95 us
    gather x1, local copies, waits for them, and re-layouts, body(): combined[indices]  4.76 us
    ppermute x2, waiting for transfers between devices, shifted(): return lax.ppermute(block, axis, route)  4.53 us
  transfers between devices with their start and end apart: 4, of which 2 were waited for; matrix products, arithmetic and copies ran while one was open for 4% of the time, Pallas kernels for 0%

commit v1 on v0

--- a/solution.py
+++ b/solution.py
@@ -80,7 +80,8 @@
     )
     coarse_share = lax.psum_scatter(assembly, "narrow", scatter_dimension=1, tiled=True)
     solved_share = coarse_solve(coarse_share, coarse_sub[0], coarse_pivot[0])
-    coarse_sol = lax.all_gather(solved_share, "narrow", axis=1, tiled=True)
+    stack = jnp.stack([solved_share] * lax.axis_size("narrow"))
+    coarse_sol = jnp.concatenate(lax.all_to_all(stack, "narrow", 0, 0), axis=1)
     coarse_vals = exact_dot(one_hot, coarse_sol)
     spread = lax.dot_general(
         basis.astype(jnp.float32),

time: 195 us -> 200 us (1.026)
  blocking collectives: 132 us -> 127 us
  waiting for transfers between devices: 4.55 us -> 9.09 us
  starting transfers between devices: 8.46 us -> 11.8 us
    all_gather x1 -> x0, blocking collectives: 5.42 us -> none  [body(): coarse_sol = lax.all_gather(solved_share, 'narrow', axis=1, tiled=True)]
    all_to_all x0 -> x1, waiting for transfers between devices: none -> 4.55 us  [body(): coarse_sol = jnp.concatenate(lax.all_to_all(stack, 'narrow', 0, 0), axis=1)]
    all_to_all x0 -> x1, starting transfers between devices: none -> 3.33 us  [body(): coarse_sol = jnp.concatenate(lax.all_to_all(stack, 'narrow', 0, 0), axis=1)]
  transfers between devices with their start and end apart: 4 -> 5, of which waited for: 2 -> 3; matrix products, arithmetic and copies ran while one was open for 4% -> 5% of each run, Pallas kernels for 0% -> 0%
where the time goes in v1:
time: 200 us
  blocking collectives  127 us (64%)
  matrix products  14 us (7%)
  other arithmetic  13.7 us (7%)
  between operations  13.6 us (7%)
  starting transfers between devices  11.8 us (6%)
  local copies, waits for them, and re-layouts  10.2 us (5%)
  waiting for transfers between devices  9.09 us (5%)
    all_gather x4, blocking collectives, entering(): gathered = jax.tree.map(lambda a: lax.all_gather(a, axis), part)  127 us
    scatter-add x1, other arithmetic, body(): summed = combined.astype(jnp.float32).at[indices.reshape(-1)].add(incomin...  11.7 us
    dot_general x1, matrix products, body(): jnp.dot(local_inverse[0, 0], weighted, preferred_element_type=jnp.float32)  6.5 us
    ppermute x2, starting transfers between devices, shifted(): return lax.ppermute(block, axis, route)  4.96 us
    gather x1, local copies, waits for them, and re-layouts, body(): combined[indices]  4.76 us
    all_to_all x1, waiting for transfers between devices, body(): coarse_sol = jnp.concatenate(lax.all_to_all(stack, 'narrow', 0, 0), axis=1)  4.55 us
    ppermute x2, waiting for transfers between devices, shifted(): return lax.ppermute(block, axis, route)  4.52 us
  transfers between devices with their start and end apart: 5, of which 3 were waited for; matrix products, arithmetic and copies ran while one was open for 5% of the time, Pallas kernels for 0%

profile of v1, /device:TPU:0, one launch (start us, length us, event | category | flops | bytes accessed | tf_op | source)
XLA Modules:
  0.0 199.7 jit_solution(13801341635899596348)
XLA Ops:
  6.5 0.9 copy-done
  7.4 1.7 fusion.15
  9.1 1.6 fusion.26
  10.8 0.9 copy.17
  11.6 0.8 neg.10
  12.5 0.7 fusion.28
  13.2 32.9 %all_gather.22 = f32[8,96,96]{2,1,0:T(8,128)S(1)} all-gather(f32[1,96,96]{2,1,0:T(8,128)S(1)} %neg.10), channel_id=1, replica_groups=mesh['wide'=8,'narrow'=4] {'wide'}, dimensions={0}, use_global_device_ids=true | all-gather | bytes 331776 | tf_op jit(solution)/shard_map/all_gather | solution.py:13
  46.1 30.9 %all-gather.1 = f32[768,96]{1,0:T(8,128)S(1)} all-gather(f32[96,96]{1,0:T(8,128)S(1)} %fusion.24), channel_id=3, replica_groups=mesh['wide'=8,'narrow'=4] {'wide'}, dimensions={0}, use_global_device_ids=true | all-gather | bytes 331776 | tf_op jit(solution)/shard_map/all_gather | solution.py:13
  77.1 6.5 %fusion.6 = f32[256,2048]{1,0:T(8,128)S(1)} fusion(bf16[1,1,2048,2048]{3,2,1,0:T(8,128)(2,1)} %param.15, bf16[1,1,2048,256]{3,2,1,0:T(8,128)(2,1)} %param.13, f32[2048]{0:T(1024)S(1)} %bitcast.99), kind=kOutput, calls=%fused_computation.10 | convolution fusion | flops 2149056512 | bytes 11542528 | tf_op jit(solution)/shard_map/dot_general | solution.py:67
  83.7 30.9 %all-gather.3 = f32[8,96,64]{1,2,0:T(8,128)S(1)} all-gather(f32[1,96,64]{1,2,0:T(8,128)} %bitcast.96), channel_id=2, replica_groups=mesh['wide'=8,'narrow'=4] {'wide'}, dimensions={0}, use_global_device_ids=true | all-gather | bytes 221184 | tf_op jit(solution)/shard_map/all_gather | solution.py:13
  114.7 1.0 fusion.13
  116.1 32.2 %all-gather.4 = f32[8,96,64]{1,2,0:T(8,128)S(1)} all-gather(f32[1,96,64]{1,2,0:T(8,128)S(1)} %convolution_bitcast_fusion), channel_id=4, replica_groups=mesh['wide'=8,'narrow'=4] {'wide'}, dimensions={0}, use_global_device_ids=true | all-gather | bytes 221184 | tf_op jit(solution)/shard_map/all_gather | solution.py:13
  148.2 1.8 while.27
  148.2 0.2 convolution_add_fusion.6
  148.5 0.2 convolution_add_fusion.6
  148.8 0.2 convolution_add_fusion.6
  149.8 0.2 convolution_add_fusion.6
  150.1 0.7 stack.2
  150.7 3.3 %all-to-all-start = ((f32[4,96,64]{1,2,0:T(8,128)}), f32[4,96,64]{1,2,0:T(8,128)S(1)}, u32[]{:S(2)}, u32[]{:S(2)}) async-start(f32[4,96,64]{1,2,0:T(8,128)} %stack.2), calls=%async_computation.1 | async-start | bytes 262144 | tf_op jit(solution)/shard_map/all_to_all | solution.py:84
  154.1 4.6 %all-to-all-done = f32[4,96,64]{1,2,0:T(8,128)S(1)} async-done(((f32[4,96,64]{1,2,0:T(8,128)}), f32[4,96,64]{1,2,0:T(8,128)S(1)}, u32[]{:S(2)}, u32[]{:S(2)}) %all-to-all-start) | async-done | bytes 98336 | tf_op jit(solution)/shard_map/all_to_all | solution.py:84
  158.8 1.1 fusion.10
  160.0 0.5 copy.18
  160.5 4.8 %gather_fusion = bf16[1536,256]{1,0:T(8,128)(2,1)S(1)} fusion(bf16[2048,256]{1,0:T(8,128)(2,1)S(1)} %copy.18, s32[2048]{0:T(1024)S(1)} %pad_clamp_fusion), kind=kCustom, calls=%fused_computation | custom fusion | bytes 1579008 | tf_op jit(solution)/shard_map/gather | solution.py:98
  165.3 0.3 broadcast_select_fusion
  165.6 0.8 slice.14
  166.4 3.5 %all-to-all-start.1 = ((bf16[4,256,256]{2,1,0:T(8,128)(2,1)}), bf16[4,256,256]{2,1,0:T(8,128)(2,1)S(1)}, u32[]{:S(2)}, u32[]{:S(2)}) async-start(bf16[4,256,256]{2,1,0:T(8,128)(2,1)} %slice.14), calls=%async_computation.2 | async-start | bytes 1048576 | tf_op jit(solution)/shard_map/all_to_all | solution.py:99
  169.9 3.7 %collective-permute-start = (bf16[256,256]{1,0:T(8,128)(2,1)S(1)}, bf16[256,256]{1,0:T(8,128)(2,1)S(1)}, u32[]{:S(2)}, u32[]{:S(2)}) collective-permute-start(bf16[256,256]{1,0:T(8,128)(2,1)S(1)} %get-tuple-element.155), channel_id=1, source_target_pairs={{0,4},{4,8},{8,12},{12,16},{16,20},{20,24},{24,28},{1,5},{5,9},{9,... | collective-permute-start | bytes 393224 | tf_op jit(solution)/shard_map/ppermute | solution.py:28
  173.6 1.3 collective-permute-start.1
  174.9 1.6 copy.19
  176.5 0.4 collective-permute-done
  176.9 4.1 %collective-permute-done.1 = bf16[256,256]{1,0:T(8,128)(2,1)S(1)} collective-permute-done((bf16[256,256]{1,0:T(8,128)(2,1)S(1)}, bf16[256,256]{1,0:T(8,128)(2,1)S(1)}, u32[]{:S(2)}, u32[]{:S(2)}) %collective-permute-start.1) | collective-permute-done | bytes 131104 | tf_op jit(solution)/shard_map/ppermute | solution.py:28
  181.2 11.7 %scatter_custom_fusion = f32[2048,256]{1,0:T(8,128)} fusion(f32[2048,256]{1,0:T(8,128)} %copy.19, s32[1536]{0:T(1024)S(1)} %fusion.27, bf16[1536,256]{1,0:T(8,128)(2,1)S(1)} %bitcast.90), kind=kCustom, calls=%fused_computation.17 | custom fusion | flops 786432 | bytes 2883584 | tf_op jit(solution)/shard_map/scatter-add | solution.py:107
  (41 shorter events, 1.6 us)
Async XLA Ops:
  6.5 0.9 copy-start
  6.5 70.5 %copy-start.4 = (f32[1,1,2048]{2,1,0:T(1,128)S(1)}, f32[1,1,2048]{2,1,0:T(1,128)}, u32[]{:S(2)}) copy-start(f32[1,1,2048]{2,1,0:T(1,128)} %param.14) | copy-start | bytes 24580
  6.5 77.2 %reduce-scatter.2.cloned.1.call-start = ((), (), s32[]{:S(2)}) async-start(), calls=%async_computation.3 | async-start | bytes 163840 | tf_op jit(solution)/shard_map/reduce_scatter | solution.py:81
  77.1 6.5 %copy-start.6 = (s32[1,1,6]{2,1,0:T(1,128)S(1)}, s32[1,1,6]{2,1,0:T(1,128)}, u32[]{:S(2)}) copy-start(s32[1,1,6]{2,1,0:T(1,128)} %param.19) | copy-start | bytes 76
  77.1 37.6 %copy-start.1 = (f32[1,96,96]{2,1,0:T(8,128)S(1)}, f32[1,96,96]{2,1,0:T(8,128)}, u32[]{:S(2)}) copy-start(f32[1,96,96]{2,1,0:T(8,128)} %param.20) | copy-start | bytes 110596
  77.1 38.6 %copy-start.2 = (f32[1,96,96]{2,1,0:T(8,128)S(1)}, f32[1,96,96]{2,1,0:T(8,128)}, u32[]{:S(2)}) copy-start(f32[1,96,96]{2,1,0:T(8,128)} %param.21) | copy-start | bytes 110596
  83.6 75.0 %copy-start.5 = (s32[1,1,24]{2,1,0:T(1,128)S(1)}, s32[1,1,24]{2,1,0:T(1,128)}, u32[]{:S(2)}) copy-start(s32[1,1,24]{2,1,0:T(1,128)} %param.17) | copy-start | bytes 292
  150.7 7.9 %all-to-all-start = ((f32[4,96,64]{1,2,0:T(8,128)}), f32[4,96,64]{1,2,0:T(8,128)S(1)}, u32[]{:S(2)}, u32[]{:S(2)}) async-start(f32[4,96,64]{1,2,0:T(8,128)} %stack.2), calls=%async_computation.1 | async-start | bytes 262144 | tf_op jit(solution)/shard_map/all_to_all | solution.py:84
  165.3 9.6 %copy-start.3 = (s32[1,1,6,256]{3,1,2,0:T(1,128)S(1)}, s32[1,1,6,256]{3,1,2,0:T(1,128)}, u32[]{:S(2)}) copy-start(s32[1,1,6,256]{3,1,2,0:T(1,128)} %param.18) | copy-start | bytes 18436
  166.4 14.7 %all-to-all-start.1 = ((bf16[4,256,256]{2,1,0:T(8,128)(2,1)}), bf16[4,256,256]{2,1,0:T(8,128)(2,1)S(1)}, u32[]{:S(2)}, u32[]{:S(2)}) async-start(bf16[4,256,256]{2,1,0:T(8,128)(2,1)} %slice.14), calls=%async_computation.2 | async-start | bytes 1048576 | tf_op jit(solution)/shard_map/all_to_all | solution.py:99
  169.9 7.0 %collective-permute-start = (bf16[256,256]{1,0:T(8,128)(2,1)S(1)}, bf16[256,256]{1,0:T(8,128)(2,1)S(1)}, u32[]{:S(2)}, u32[]{:S(2)}) collective-permute-start(bf16[256,256]{1,0:T(8,128)(2,1)S(1)} %get-tuple-element.155), channel_id=1, source_target_pairs={{0,4},{4,8},{8,12},{12,16},{16,20},{20,24},{24,28},{1,5},{5,9},{9,... | collective-permute-start | bytes 393224 | tf_op jit(solution)/shard_map/ppermute | solution.py:28
  173.6 7.5 %collective-permute-start.1 = (bf16[256,256]{1,0:T(8,128)(2,1)S(1)}, bf16[256,256]{1,0:T(8,128)(2,1)S(1)}, u32[]{:S(2)}, u32[]{:S(2)}) collective-permute-start(bf16[256,256]{1,0:T(8,128)(2,1)S(1)} %get-tuple-element.156), channel_id=1, source_target_pairs={{4,0},{8,4},{12,8},{16,12},{20,16},{24,20},{28,24},{5,1},{9,5},{13... | collective-permute-start | bytes 393224 | tf_op jit(solution)/shard_map/ppermute | solution.py:28
Sparse Core Ops, SparseCore 0:
  10.9 22.3 reduce-scatter.1
